TPU v7x, 32 devices: a whole 2x2x4 slice. The times are simulated.
32 devices in a mesh: group: 2 (over y), tm: 4 (over x, core), space: 4 (over z).
Axes of the slice: x: 2, y: 2, z: 4, core: 2. Of those that a mesh axis runs over, the one named last changes fastest.
Arguments:
- latent: bfloat16 [8, 16, 4, 128], P(('group', 'tm'), None, 'space'), parts along dimension 0, may hold values from -27 to 27
- conv_weight: bfloat16 [3, 3, 3, 16, 512], replicated, may hold values from -0.3125 to 0.3125
- norm_gain: float32 [512], replicated, may hold values from 0.25 to 1.75
- qkv_weight: bfloat16 [512, 1536], replicated, may hold values from -0.25 to 0.25
- out_weight: bfloat16 [512, 512], replicated, may hold values from -0.25 to 0.25
- grad_out: bfloat16 [8, 4, 128, 512], P(('group', 'tm'), 'space'), parts along dimension 0, may hold values from -6 to 6
Outputs:
- grad_latent: float32 [8, 16, 4, 128], P(('group', 'tm'), None, 'space'), parts along dimension 0
There are 2 independent parts, one for each index of `group`. A program takes and returns all parts, laid end to end along the dimension named above; an argument that names none is the same for every part. Nothing has to cross between parts.
All inputs are finite; a program needn't handle non-finite values.
Results may differ from a plain program's by a relative error of at most 0.013.
The roundings to bfloat16 on the way count: a program that leaves them out, or rounds other values in their place, can miss the bound.
Values may be sent and summed in bfloat16 or wider, within the bound.
A program may use at most 64 MiB of HBM per device.

v0:
```python
import jax
import jax.numpy as jnp
from jax import lax
from jax.sharding import PartitionSpec as P

GROUPS = 32


EPSILON = 1e-06


def from_behind(value, axis, steps):
    count = lax.axis_size(axis)
    leading, last = (max(0, -steps), min(count, count - steps))
    return lax.ppermute(value, axis, [(source, source + steps) for source in range(leading, last)])


def padded_2(value, sides, width):
    for axis, dim in sides:
        count, length = (lax.axis_size(axis), value.shape[dim])
        up = [(i, (i + 1) % count) for i in range(count - 1)]
        down = [(j, i) for i, j in up]
        last = lax.slice_in_dim(value, length - width, length, axis=dim)
        leading = lax.slice_in_dim(value, 0, width, axis=dim)
        before = lax.ppermute(last, axis, up)
        after = lax.ppermute(leading, axis, down)
        value = jnp.concatenate([before, value, after], axis=dim)
    return value


def contract(left, right, left_dim, right_dim):
    return lax.dot_general(
        left, right, (((left_dim,), (right_dim,)), ((), ())), preferred_element_type=jnp.float32
    )


def on_device(latent, conv_weight, norm_gain, qkv_weight, out_weight, grad_out):
    lat_width = latent.shape[1]
    row_count = latent.shape[2]
    col_count = latent.shape[3]
    channels = grad_out.shape[3]
    cells = row_count * col_count
    per_group = channels // GROUPS
    scaling = channels ** (-0.5)
    conv_flat = conv_weight.reshape(27 * lat_width, channels)
    far_frame = from_behind(latent, "tm", 2)
    near_frame = from_behind(latent, "tm", 1)
    window = jnp.concatenate([far_frame, near_frame, latent], axis=0)
    haloed = padded_2(window, (("space", 2),), 1)
    padded = jnp.pad(haloed, ((0, 0), (0, 0), (0, 0), (1, 1)))
    pieces = []
    for a in range(3):
        for b in range(3):
            for e in range(3):
                pieces.append(padded[2 - a, :, b : b + row_count, e : e + col_count])
    patches = jnp.concatenate(pieces, axis=0).reshape(27 * lat_width, cells)
    hidden = contract(patches, conv_flat, 0, 0)
    grouped = hidden.reshape(cells, GROUPS, per_group)
    count_all = float(lax.axis_size("space") * cells * per_group)
    sum_plain, sum_square = lax.psum(
        (jnp.sum(grouped, axis=(0, 2)), jnp.sum(grouped * grouped, axis=(0, 2))), "space"
    )
    average = sum_plain / count_all
    spread = sum_square / count_all - average * average
    inverse = lax.rsqrt(spread + EPSILON)
    unit_cells = (grouped - average[None, :, None]) * inverse[None, :, None]
    gain_grid = norm_gain.reshape(GROUPS, per_group)
    normed = (unit_cells * gain_grid).astype(jnp.bfloat16).reshape(cells, channels)
    projected = jnp.dot(normed, qkv_weight, preferred_element_type=jnp.float32).astype(jnp.bfloat16)
    query_part = projected[:, :channels]
    key_part = projected[:, channels : 2 * channels]
    value_part = projected[:, 2 * channels :]
    upstream = grad_out.reshape(cells, channels)
    grad_att = contract(upstream, out_weight, 1, 1).astype(jnp.bfloat16)
    largest = jnp.full((cells,), -1e30, jnp.float32)
    scores = (
        contract(query_part, lax.all_gather(key_part, "space", axis=0, tiled=True), 1, 1) * scaling
    )
    highest = jnp.maximum(largest, jnp.max(scores, axis=1))
    running = jnp.sum(jnp.exp(scores - highest[:, None]), axis=1)
    largest, running = (highest, running)
    log_norm = largest + jnp.log(running)
    key_piece = lax.all_gather(key_part, "space", axis=0, tiled=True)
    value_piece = lax.all_gather(value_part, "space", axis=0, tiled=True)
    scores = contract(query_part, key_piece, 1, 1) * scaling
    soft_bf = jnp.exp(scores - log_norm[:, None]).astype(jnp.bfloat16)
    attended = jnp.dot(soft_bf, value_piece, preferred_element_type=jnp.float32)
    attended = lax.optimization_barrier(attended.astype(jnp.bfloat16))
    row_delta = jnp.sum(grad_att.astype(jnp.float32) * attended.astype(jnp.float32), axis=1)
    key_piece = lax.all_gather(key_part, "space", axis=0, tiled=True)
    value_piece = lax.all_gather(value_part, "space", axis=0, tiled=True)
    scores = contract(query_part, key_piece, 1, 1) * scaling
    soft_probs = jnp.exp(scores - log_norm[:, None])
    grad_probs = contract(grad_att, value_piece, 1, 1)
    dscore = (soft_probs * (grad_probs - row_delta[:, None]) * scaling).astype(jnp.bfloat16)
    grad_query = jnp.dot(dscore, key_piece, preferred_element_type=jnp.float32).astype(jnp.bfloat16)
    all_norms, all_deltas = (
        lax.all_gather(log_norm, "space", axis=0, tiled=True),
        lax.all_gather(row_delta, "space", axis=0, tiled=True),
    )
    query_piece = lax.all_gather(query_part, "space", axis=0, tiled=True)
    grad_piece = lax.all_gather(grad_att, "space", axis=0, tiled=True)
    scores = contract(query_piece, key_part, 1, 1) * scaling
    soft_probs = jnp.exp(scores - all_norms[:, None])
    soft_bf = soft_probs.astype(jnp.bfloat16)
    grad_probs = contract(grad_piece, value_part, 1, 1)
    dscore = (soft_probs * (grad_probs - all_deltas[:, None]) * scaling).astype(jnp.bfloat16)
    key_accum = contract(dscore, query_piece, 0, 0)
    value_accum = contract(soft_bf, grad_piece, 0, 0)
    grad_proj = jnp.concatenate(
        [grad_query, key_accum.astype(jnp.bfloat16), value_accum.astype(jnp.bfloat16)], axis=1
    )
    grad_normed = contract(grad_proj, qkv_weight, 1, 1)
    scaled = grad_normed.reshape(cells, GROUPS, per_group) * gain_grid
    grad_first, grad_second = lax.psum(
        (jnp.sum(scaled, axis=(0, 2)), jnp.sum(scaled * unit_cells, axis=(0, 2))), "space"
    )
    first_mean = grad_first / count_all
    second_mean = grad_second / count_all
    grad_hidden = upstream.astype(jnp.float32).reshape(cells, GROUPS, per_group)
    grad_hidden = (
        grad_hidden
        + (scaled - first_mean[None, :, None] - unit_cells * second_mean[None, :, None])
        * inverse[None, :, None]
    )
    grad_hidden = grad_hidden.astype(jnp.bfloat16).reshape(1, row_count, col_count, channels)
    after_one = from_behind(grad_hidden, "tm", -1)
    after_two = from_behind(grad_hidden, "tm", -2)
    window_grad = jnp.concatenate([grad_hidden, after_one, after_two], axis=0)
    haloed_grad = padded_2(window_grad, (("space", 1),), 1)
    summed = jnp.zeros((lat_width, row_count, col_count), jnp.float32)
    tap_rows = 9 * lat_width
    for a in range(3):
        columns = contract(
            conv_flat[a * tap_rows : (a + 1) * tap_rows], haloed_grad[a].reshape(-1, channels), 1, 1
        )
        columns = columns.reshape(3, 3, lat_width, row_count + 2, col_count)
        columns = jnp.pad(columns, ((0, 0), (0, 0), (0, 0), (0, 0), (1, 1)))
        for b in range(3):
            for e in range(3):
                summed = (
                    summed + columns[b, e, :, 2 - b : 2 - b + row_count, 2 - e : 2 - e + col_count]
                )
    return summed[None]


def solution(mesh):
    return jax.shard_map(
        on_device,
        mesh=mesh,
        in_specs=(
            P(("group", "tm"), None, "space", None),
            P(),
            P(),
            P(),
            P(),
            P(("group", "tm"), "space", None, None),
        ),
        out_specs=P(("group", "tm"), None, "space", None),
        check_vma=False,
    )
```

profile of v0, /device:TPU:0, one launch (start us, length us, event | category | flops | bytes accessed | tf_op | source)
XLA Modules:
  0.0 157.7 jit_solution(4442520707237397019)
XLA Ops:
  0.0 5.0 %collective-permute-start = (bf16[1,16,1,128]{3,1,2,0:T(8,128)(2,1)}, bf16[1,16,1,128]{3,1,2,0:T(8,128)(2,1)S(1)}, u32[]{:S(2)}, u32[]{:S(2)}) collective-permute-start(bf16[1,16,1,128]{3,1,2,0:T(8,128)(2,1)} %param.6), channel_id=1, source_target_pairs={{0,8},{4,12},{1,9},{5,13},{2,10},{6,14},{3,11},{7,15},{16,24},{20,... | collective-permute-start | bytes 12296 | tf_op jit(solution)/shard_map/ppermute | solution.py:15
  5.0 1.5 collective-permute-start.1
  6.5 1.0 collective-permute-done.1
  7.5 0.7 constant_dynamic-update-slice_fusion
  8.2 3.5 %collective-permute-start.2 = (bf16[3,16,1,128]{3,1,2,0:T(8,128)(2,1)S(1)}, bf16[3,16,1,128]{3,1,2,0:T(8,128)(2,1)S(1)}, u32[]{:S(2)}, u32[]{:S(2)}) collective-permute-start(bf16[3,16,1,128]{3,1,2,0:T(8,128)(2,1)S(1)} %constant_dynamic-update-slice_fusion), channel_id=1, source_target_pairs={{0,1},{1,2},{2,3},{4,5},{5,6},{6,7},{8,9},{9,10},{10,11},{12,13},{... | collective-permute-start | bytes 36872 | tf_op jit(solution)/shard_map/ppermute | solution.py:25
  11.6 1.3 collective-permute-start.3
  12.9 1.2 copy.87
  14.2 0.8 mul.79
  15.0 1.0 copy.86
  16.0 0.7 convert.1
  16.8 0.5 collective-permute-done.3
  18.2 0.6 fusion.74
  18.8 12.6 %all-reduce.5 = (f32[32]{0:T(128)S(1)}, f32[32]{0:T(128)S(1)}) all-reduce(f32[32]{0:T(128)S(1)} %get-tuple-element.6, f32[32]{0:T(128)S(1)} %get-tuple-element.5), channel_id=1, replica_groups=mesh['group'=2,'tm'=4,'space'=4] {'space'}, use_global_device_ids=true, to_apply=%region_3.4 | all-reduce | flops 64 | bytes 512 | tf_op jit(solution)/shard_map/psum | solution.py:60
  31.6 0.4 convolution_convert_fusion
  32.0 0.7 fusion.77
  32.8 14.8 %all_gather.21 = bf16[512,512]{1,0:T(8,128)(2,1)S(1)} all-gather(bf16[128,512]{1,0:T(8,128)(2,1)S(1)} %get-tuple-element.18), channel_id=1, replica_groups=mesh['group'=2,'tm'=4,'space'=4] {'space'}, dimensions={0}, use_global_device_ids=true | all-gather | bytes 655360 | tf_op jit(solution)/shard_map/all_gather | solution.py:90
  47.6 0.4 fusion.78
  48.0 0.2 exponential_reduce_fusion
  48.2 15.7 %all_gather.22 = bf16[512,512]{1,0:T(8,128)(2,1)S(1)} all-gather(bf16[128,512]{1,0:T(8,128)(2,1)S(1)} %get-tuple-element.17), channel_id=1, replica_groups=mesh['group'=2,'tm'=4,'space'=4] {'space'}, dimensions={0}, use_global_device_ids=true | all-gather | bytes 655360 | tf_op jit(solution)/shard_map/all_gather | solution.py:91
  63.9 0.3 convolution_convert_fusion.4
  64.2 0.9 multiply_reduce_fusion.2
  65.1 14.7 %all_gather.25 = bf16[512,512]{1,0:T(8,128)(2,1)S(1)} all-gather(bf16[128,512]{1,0:T(8,128)(2,1)S(1)} %get-tuple-element.26), channel_id=1, replica_groups=mesh['group'=2,'tm'=4,'space'=4] {'space'}, dimensions={0}, use_global_device_ids=true | all-gather | bytes 655360 | tf_op jit(solution)/shard_map/all_gather | solution.py:102
  79.8 1.8 %convolution_convert_fusion.3 = bf16[128,512]{1,0:T(8,128)(2,1)} fusion(bf16[512,512]{1,0:T(8,128)(2,1)S(1)} %all_gather.21, bf16[128,512]{1,0:T(8,128)(2,1)S(1)} %get-tuple-element.26, bf16[512,512]{1,0:T(8,128)(2,1)S(1)} %all_gather.22, f32[128,512]{1,0:T(8,128)S(1)} %get-tuple-element.24, f32[128]{0:T(128)} %get-tuple-element.25, f32[128]{0:T(128)} %copy-done.11), kind=kOutput, calls=%fused_computation.17 | convolution fusion | flops 134610944 | bytes 1573888 | tf_op jit(solution)/shard_map/dot_general | solution.py:96
  81.6 9.7 %all-gather = f32[4,1,128]{2,1,0:T(1,128)S(1)} all-gather(f32[1,1,128]{2,1,0:T(1,128)} %bitcast.260), channel_id=1, replica_groups=mesh['group'=2,'tm'=4,'space'=4] {'space'}, dimensions={0}, use_global_device_ids=true | all-gather | bytes 2560 | tf_op jit(solution)/shard_map/all_gather | solution.py:98
  91.3 14.9 %all_gather.23 = bf16[512,512]{1,0:T(8,128)(2,1)S(1)} all-gather(bf16[128,512]{1,0:T(8,128)(2,1)} %get-tuple-element.19), channel_id=1, replica_groups=mesh['group'=2,'tm'=4,'space'=4] {'space'}, dimensions={0}, use_global_device_ids=true | all-gather | bytes 655360 | tf_op jit(solution)/shard_map/all_gather | solution.py:101
  106.2 8.0 %all-gather.1 = f32[4,1,128]{2,1,0:T(1,128)S(1)} all-gather(f32[1,1,128]{2,1,0:T(1,128)} %bitcast.261), channel_id=1, replica_groups=mesh['group'=2,'tm'=4,'space'=4] {'space'}, dimensions={0}, use_global_device_ids=true | all-gather | bytes 2560 | tf_op jit(solution)/shard_map/all_gather | solution.py:99
  114.2 1.2 fusion.2
  115.5 0.2 convolution_convert_fusion.1
  115.7 1.5 convolution_convert_fusion.2
  117.3 0.7 multiply_reduce_fusion.1
  118.2 0.2 multiply_reduce_fusion
  118.7 10.0 %all-reduce.4 = (f32[32]{0:T(128)S(1)}, f32[32]{0:T(128)S(1)}) all-reduce(f32[32]{0:T(128)S(1)} %multiply_reduce_fusion, f32[32]{0:T(128)S(1)} %reduce_sum.67), channel_id=1, replica_groups=mesh['group'=2,'tm'=4,'space'=4] {'space'}, use_global_device_ids=true, to_apply=%region_11.12 | all-reduce | flops 64 | bytes 512 | tf_op jit(solution)/shard_map/psum | solution.py:115
  128.7 0.2 fusion.16
  129.0 1.3 collective-permute-start.4
  130.3 1.3 collective-permute-start.5
  131.6 0.6 collective-permute-done.4
  132.3 6.2 %collective-permute-done.5 = bf16[1,1,128,512]{2,3,1,0:T(8,128)(2,1)S(1)} collective-permute-done((bf16[1,1,128,512]{2,3,1,0:T(8,128)(2,1)S(1)}, bf16[1,1,128,512]{2,3,1,0:T(8,128)(2,1)S(1)}, u32[]{:S(2)}, u32[]{:S(2)}) %collective-permute-start.5) | collective-permute-done | bytes 131104 | tf_op jit(solution)/shard_map/ppermute | solution.py:15
  138.5 3.0 %collective-permute-start.6 = (bf16[3,1,128,512]{2,3,1,0:T(8,128)(2,1)S(1)}, bf16[3,1,128,512]{2,3,1,0:T(8,128)(2,1)S(1)}, u32[]{:S(2)}, u32[]{:S(2)}) collective-permute-start(bf16[3,1,128,512]{2,3,1,0:T(8,128)(2,1)S(1)} %pad_maximum_fusion.1), channel_id=1, source_target_pairs={{0,1},{1,2},{2,3},{4,5},{5,6},{6,7},{8,9},{9,10},{10,11},{12,13},{... | collective-permute-start | bytes 1179656 | tf_op jit(solution)/shard_map/ppermute | solution.py:25
  141.5 1.3 collective-permute-start.7
  142.8 0.7 fusion.76
  143.5 6.3 %collective-permute-done.6 = bf16[3,1,128,512]{2,3,1,0:T(8,128)(2,1)S(1)} collective-permute-done((bf16[3,1,128,512]{2,3,1,0:T(8,128)(2,1)S(1)}, bf16[3,1,128,512]{2,3,1,0:T(8,128)(2,1)S(1)}, u32[]{:S(2)}, u32[]{:S(2)}) %collective-permute-start.6) | collective-permute-done | bytes 393248 | tf_op jit(solution)/shard_map/ppermute | solution.py:25
  149.8 4.1 %collective-permute-done.7 = bf16[3,1,128,512]{2,3,1,0:T(8,128)(2,1)S(1)} collective-permute-done((bf16[3,1,128,512]{2,3,1,0:T(8,128)(2,1)S(1)}, bf16[3,1,128,512]{2,3,1,0:T(8,128)(2,1)S(1)}, u32[]{:S(2)}, u32[]{:S(2)}) %collective-permute-start.7) | collective-permute-done | bytes 393248 | tf_op jit(solution)/shard_map/ppermute | solution.py:26
  154.2 0.2 copy.100
  154.4 1.2 convolution_bitcast_fusion.1
  155.7 0.2 copy.105
  155.9 0.3 convolution_bitcast_fusion
  156.6 0.3 convolution_bitcast_fusion.2
  157.0 0.7 fusion.63
  (79 shorter events, 2.6 us)
Async XLA Ops:
  0.0 31.6 %copy-start = (bf16[512,1536]{1,0:T(8,128)(2,1)S(1)}, bf16[512,1536]{1,0:T(8,128)(2,1)}, u32[]{:S(2)}) copy-start(bf16[512,1536]{1,0:T(8,128)(2,1)} %param.9) | copy-start | bytes 4718596
  0.0 17.4 %copy-start.10 = (bf16[1,16,1,128]{3,1,2,0:T(8,128)(2,1)S(1)}, bf16[1,16,1,128]{3,1,2,0:T(8,128)(2,1)}, u32[]{:S(2)}) copy-start(bf16[1,16,1,128]{3,1,2,0:T(8,128)(2,1)} %param.6) | copy-start | bytes 12292
  0.0 6.5 %collective-permute-start = (bf16[1,16,1,128]{3,1,2,0:T(8,128)(2,1)}, bf16[1,16,1,128]{3,1,2,0:T(8,128)(2,1)S(1)}, u32[]{:S(2)}, u32[]{:S(2)}) collective-permute-start(bf16[1,16,1,128]{3,1,2,0:T(8,128)(2,1)} %param.6), channel_id=1, source_target_pairs={{0,8},{4,12},{1,9},{5,13},{2,10},{6,14},{3,11},{7,15},{16,24},{20,... | collective-permute-start | bytes 12296 | tf_op jit(solution)/shard_map/ppermute | solution.py:15
  5.0 2.5 %collective-permute-start.1 = (bf16[1,16,1,128]{3,1,2,0:T(8,128)(2,1)}, bf16[1,16,1,128]{3,1,2,0:T(8,128)(2,1)S(1)}, u32[]{:S(2)}, u32[]{:S(2)}) collective-permute-start(bf16[1,16,1,128]{3,1,2,0:T(8,128)(2,1)} %param.6), channel_id=1, source_target_pairs={{0,4},{4,8},{8,12},{1,5},{5,9},{9,13},{2,6},{6,10},{10,14},{3,7},{... | collective-permute-start | bytes 12296 | tf_op jit(solution)/shard_map/ppermute | solution.py:15
  8.2 8.6 %collective-permute-start.2 = (bf16[3,16,1,128]{3,1,2,0:T(8,128)(2,1)S(1)}, bf16[3,16,1,128]{3,1,2,0:T(8,128)(2,1)S(1)}, u32[]{:S(2)}, u32[]{:S(2)}) collective-permute-start(bf16[3,16,1,128]{3,1,2,0:T(8,128)(2,1)S(1)} %constant_dynamic-update-slice_fusion), channel_id=1, source_target_pairs={{0,1},{1,2},{2,3},{4,5},{5,6},{6,7},{8,9},{9,10},{10,11},{12,13},{... | collective-permute-start | bytes 36872 | tf_op jit(solution)/shard_map/ppermute | solution.py:25
  11.6 5.6 %collective-permute-start.3 = (bf16[3,16,1,128]{3,1,2,0:T(8,128)(2,1)S(1)}, bf16[3,16,1,128]{3,1,2,0:T(8,128)(2,1)S(1)}, u32[]{:S(2)}, u32[]{:S(2)}) collective-permute-start(bf16[3,16,1,128]{3,1,2,0:T(8,128)(2,1)S(1)} %constant_dynamic-update-slice_fusion), channel_id=1, source_target_pairs={{1,0},{2,1},{3,2},{5,4},{6,5},{7,6},{9,8},{10,9},{11,10},{13,12},{... | collective-permute-start | bytes 36872 | tf_op jit(solution)/shard_map/ppermute | solution.py:26
  18.8 13.2 %copy-start.2 = (f32[128,32,16]{0,1,2:T(8,128)}, f32[128,32,16]{0,1,2:T(8,128)S(1)}, u32[]{:S(2)}) copy-start(f32[128,32,16]{0,1,2:T(8,128)S(1)} %get-tuple-element.22) | copy-start | bytes 786436
  32.0 15.9 %copy-start.1 = (bf16[128,1536]{1,0:T(8,128)(2,1)}, bf16[128,1536]{1,0:T(8,128)(2,1)S(1)}, u32[]{:S(2)}) copy-start(bf16[128,1536]{1,0:T(8,128)(2,1)S(1)} %convolution_convert_fusion) | copy-start | bytes 1179652
  47.6 16.6 %copy-start.7 = (bf16[1,1,128,512]{3,2,1,0:T(8,128)(2,1)S(1)}, bf16[1,1,128,512]{3,2,1,0:T(8,128)(2,1)}, u32[]{:S(2)}) copy-start(bf16[1,1,128,512]{3,2,1,0:T(8,128)(2,1)} %param.11) | copy-start | bytes 393220
  47.6 16.7 %copy-start.8 = (bf16[512,512]{1,0:T(8,128)(2,1)S(1)}, bf16[512,512]{1,0:T(8,128)(2,1)}, u32[]{:S(2)}) copy-start(bf16[512,512]{1,0:T(8,128)(2,1)} %param.10) | copy-start | bytes 1572868
  48.2 15.8 %copy-start.11 = (f32[128]{0:T(128)}, f32[128]{0:T(128)S(1)}, u32[]{:S(2)}) copy-start(f32[128]{0:T(128)S(1)} %log_add_fusion) | copy-start | bytes 1540
  115.4 1.8 %copy-start.9 = (bf16[128,512]{1,0:T(8,128)(2,1)S(1)}, bf16[128,512]{1,0:T(8,128)(2,1)}, u32[]{:S(2)}) copy-start(bf16[128,512]{1,0:T(8,128)(2,1)} %convolution_convert_fusion.3) | copy-start | bytes 393220
  115.4 1.8 %copy-start.12 = (f32[512]{0:T(512)S(1)}, f32[512]{0:T(512)}, u32[]{:S(2)}) copy-start(f32[512]{0:T(512)} %param.8) | copy-start | bytes 6148
  117.3 1.0 copy-start.3
  117.9 10.8 %copy-start.5 = (f32[128,32,16]{0,2,1:T(8,128)S(1)}, f32[128,32,16]{0,2,1:T(8,128)}, u32[]{:S(2)}) copy-start(f32[128,32,16]{0,2,1:T(8,128)} %convert.1) | copy-start | bytes 786436
  118.2 24.6 %copy-start.4 = (bf16[3,3,3,16,512]{4,3,2,1,0:T(8,128)(2,1)S(1)}, bf16[3,3,3,16,512]{4,3,2,1,0:T(8,128)(2,1)}, u32[]{:S(2)}) copy-start(bf16[3,3,3,16,512]{4,3,2,1,0:T(8,128)(2,1)} %param.7) | copy-start | bytes 1327108
  129.0 3.2 %collective-permute-start.4 = (bf16[1,1,128,512]{2,3,1,0:T(8,128)(2,1)S(1)}, bf16[1,1,128,512]{2,3,1,0:T(8,128)(2,1)S(1)}, u32[]{:S(2)}, u32[]{:S(2)}) collective-permute-start(bf16[1,1,128,512]{2,3,1,0:T(8,128)(2,1)S(1)} %bitcast.248), channel_id=1, source_target_pairs={{4,0},{8,4},{12,8},{5,1},{9,5},{13,9},{6,2},{10,6},{14,10},{7,3},{... | collective-permute-start | bytes 393224 | tf_op jit(solution)/shard_map/ppermute | solution.py:15
  130.3 8.1 %collective-permute-start.5 = (bf16[1,1,128,512]{2,3,1,0:T(8,128)(2,1)S(1)}, bf16[1,1,128,512]{2,3,1,0:T(8,128)(2,1)S(1)}, u32[]{:S(2)}, u32[]{:S(2)}) collective-permute-start(bf16[1,1,128,512]{2,3,1,0:T(8,128)(2,1)S(1)} %bitcast.249), channel_id=1, source_target_pairs={{8,0},{12,4},{9,1},{13,5},{10,2},{14,6},{11,3},{15,7},{24,16},{28,... | collective-permute-start | bytes 393224 | tf_op jit(solution)/shard_map/ppermute | solution.py:15
  138.5 11.3 %collective-permute-start.6 = (bf16[3,1,128,512]{2,3,1,0:T(8,128)(2,1)S(1)}, bf16[3,1,128,512]{2,3,1,0:T(8,128)(2,1)S(1)}, u32[]{:S(2)}, u32[]{:S(2)}) collective-permute-start(bf16[3,1,128,512]{2,3,1,0:T(8,128)(2,1)S(1)} %pad_maximum_fusion.1), channel_id=1, source_target_pairs={{0,1},{1,2},{2,3},{4,5},{5,6},{6,7},{8,9},{9,10},{10,11},{12,13},{... | collective-permute-start | bytes 1179656 | tf_op jit(solution)/shard_map/ppermute | solution.py:25
  141.5 12.5 %collective-permute-start.7 = (bf16[3,1,128,512]{2,3,1,0:T(8,128)(2,1)S(1)}, bf16[3,1,128,512]{2,3,1,0:T(8,128)(2,1)S(1)}, u32[]{:S(2)}, u32[]{:S(2)}) collective-permute-start(bf16[3,1,128,512]{2,3,1,0:T(8,128)(2,1)S(1)} %pad_maximum_fusion.1), channel_id=1, source_target_pairs={{1,0},{2,1},{3,2},{5,4},{6,5},{7,6},{9,8},{10,9},{11,10},{13,12},{... | collective-permute-start | bytes 1179656 | tf_op jit(solution)/shard_map/ppermute | solution.py:26
  154.4 1.6 copy-start.6
where the time goes:
time: 158 us
  blocking collectives  100 us (63%)
  waiting for transfers between devices  18.7 us (12%)
  starting transfers between devices  18.1 us (11%)
  matrix products  9.75 us (6%)
  local copies, waits for them, and re-layouts  7.57 us (5%)
  other arithmetic  2.69 us (2%)
    all_gather x1, blocking collectives, on_device(): value_piece = lax.all_gather(value_part, 'space', axis=0, tiled=True)  15.7 us
    all_gather x1, blocking collectives, on_device(): query_piece = lax.all_gather(query_part, 'space', axis=0, tiled=True)  14.9 us
    all_gather x1, blocking collectives, on_device(): key_piece = lax.all_gather(key_part, 'space', axis=0, tiled=True)  14.8 us
    all_gather x1, blocking collectives, on_device(): grad_piece = lax.all_gather(grad_att, 'space', axis=0, tiled=True)  14.7 us
    psum x1, blocking collectives, on_device(): lax.psum((jnp.sum(grouped, axis=(0, 2)), jnp.sum(grouped * grouped, axis=...  12.6 us
    psum x1, blocking collectives, on_device(): lax.psum((jnp.sum(scaled, axis=(0, 2)), jnp.sum(scaled * unit_cells, axis...  10 us
    all_gather x1, blocking collectives, on_device(): lax.all_gather(log_norm, 'space', axis=0, tiled=True)  9.7 us
    ppermute x4, starting transfers between devices, from_behind(): lax.ppermute(value, axis, [(source, source + steps) for source in range(l...  9.01 us
  transfers between devices with their start and end apart: 8, of which 7 were waited for; matrix products, arithmetic and copies ran while one was open for 3% of the time, Pallas kernels for 0%

commit v1 on v0

v1 whole, which is shorter than its diff:
```python
import functools

import jax
import jax.numpy as jnp
from jax import lax
from jax.experimental import pallas as pl
from jax.experimental.pallas import tpu as pltpu
from jax.sharding import PartitionSpec as P

GROUPS = 32
EPSILON = 1e-06
BACK = 3
LANES = 128
MESH = pl.DeviceIdType.MESH


def dot(left, right, left_dim, right_dim):
    return lax.dot_general(
        left, right, (((left_dim,), (right_dim,)), ((), ())), preferred_element_type=jnp.float32
    )


def group_sums(rows, per_group):
    channels = rows[0].shape[1]
    tiles = channels // LANES
    packed = jnp.concatenate(
        [row[:, k * LANES : (k + 1) * LANES] for row in rows for k in range(tiles)], axis=0
    )
    lane = lax.broadcasted_iota(jnp.int32, packed.shape, 1)
    step = 1
    while step < per_group:
        upper = pltpu.roll(packed, step, 1)
        lower = pltpu.roll(packed, LANES - step, 1)
        packed = packed + jnp.where((lane & step) != 0, upper, lower)
        step *= 2
    return [
        jnp.concatenate([packed[i * tiles + k : i * tiles + k + 1] for k in range(tiles)], axis=1)
        for i in range(len(rows))
    ]


def shifted(value, by):
    if by == 0:
        return value
    lane = lax.broadcasted_iota(jnp.int32, value.shape, 1)
    keep = lane < LANES - 1 if by == 1 else lane > 0
    return jnp.where(keep, pltpu.roll(value, (-by) % LANES, 1), 0.0)


def chunked(count, body, carry):
    if count == 1:
        return body(0, carry)
    return lax.fori_loop(0, count, body, carry)


def kernel(
    frames, rows, chunk,
    lat_hbm, conv_hbm, gain_hbm, qkv_hbm, out_hbm, grad_hbm,
    result_ref,
    lat, conv, gain, qkv, outw, grad,
    window, patches, unit, normed, keyval, scores, products, soft, dscore, grad_kv, grad_norm,
    grad_hid, columns, partial, arrived,
    load_sem, lat_send, lat_recv, part_send, part_recv,
):
    t = lax.axis_index("tm")
    me = lax.axis_index("space")
    lat_width = lat.shape[0]
    channels = grad.shape[1]
    per_group = channels // GROUPS
    cells = rows * LANES
    chunks = cells // chunk
    scaling = channels ** (-0.5)
    own = pl.ds(pl.multiple_of(me * LANES, LANES), LANES)

    loads = [
        pltpu.make_async_copy(source, target, load_sem.at[i])
        for i, (source, target) in enumerate(
            [(lat_hbm, lat), (grad_hbm, grad), (out_hbm, outw), (conv_hbm, conv), (gain_hbm, gain), (qkv_hbm, qkv)]
        )
    ]
    for load in loads:
        load.start()

    barrier = pltpu.get_barrier_semaphore()
    for step in range(1 - BACK, BACK):
        for d in range(rows):
            if step == 0 and d == 0:
                continue

            @pl.when((t + step >= 0) & (t + step < frames))
            def _(step=step, d=d):
                pl.semaphore_signal(
                    barrier, inc=1,
                    device_id={"tm": t + step, "space": lax.rem(me + d, rows)},
                    device_id_type=MESH,
                )

    loads[0].wait()
    window[0, me] = lat[...]
    for a in range(1, BACK):

        @pl.when(t < a)
        def _(a=a):
            window[a] = jnp.zeros(window.shape[1:], window.dtype)

    near = jnp.minimum(t, BACK - 1) + jnp.minimum(frames - 1 - t, BACK - 1) + 1
    pl.semaphore_wait(barrier, near * rows - 1)

    def latent_copy(a, row, slot):
        return pltpu.make_async_remote_copy(
            src_ref=lat,
            dst_ref=window.at[a, slot],
            send_sem=lat_send.at[a, row],
            recv_sem=lat_recv.at[a, slot],
            device_id={"tm": t + a, "space": row},
            device_id_type=MESH,
        )

    pairs = [(a, d) for a in range(BACK) for d in range(rows) if a or d]
    for a, d in pairs:

        @pl.when(t + a < frames)
        def _(a=a, d=d):
            latent_copy(a, lax.rem(me + d, rows), me).start()

    loads[1].wait()
    loads[2].wait()
    grad_att = dot(grad[...], outw[...], 1, 1).astype(jnp.bfloat16)

    for a, d in pairs:

        @pl.when(t >= a)
        def _(a=a, d=d):
            slot = lax.rem(me + d, rows)
            latent_copy(a, slot, slot).wait_recv()

    zero_slab = jnp.zeros((3 * lat_width, LANES), jnp.bfloat16)
    for a in range(BACK):
        for r in range(rows):
            piece = window[a, r].astype(jnp.float32)
            for e in range(3):
                moved = shifted(piece, e - 1).astype(jnp.bfloat16)
                for b in range(3):
                    target = r - b + 1
                    if 0 <= target < rows:
                        tap = (a * 9 + b * 3 + e) * lat_width
                        patches[tap : tap + lat_width, target * LANES : (target + 1) * LANES] = moved
        first = a * 9 * lat_width
        patches[first : first + 3 * lat_width, 0:LANES] = zero_slab
        last = (a * 9 + 6) * lat_width
        patches[last : last + 3 * lat_width, (rows - 1) * LANES : rows * LANES] = zero_slab

    loads[3].wait()
    loads[4].wait()

    def rows_of(i):
        if isinstance(i, int):
            return pl.ds(i * chunk, chunk)
        return pl.ds(pl.multiple_of(i * chunk, chunk), chunk)

    zero_row = jnp.zeros((1, channels), jnp.float32)

    def convolve(i, total):
        part = dot(patches[:, rows_of(i)], conv[...], 0, 0)
        unit[rows_of(i), :] = part
        return total + jnp.sum(part, axis=0, keepdims=True)

    count = float(cells * per_group)
    (average,) = group_sums([chunked(chunks, convolve, zero_row)], per_group)
    average = average / count

    def square(i, total):
        away = unit[rows_of(i), :] - average
        return total + jnp.sum(away * away, axis=0, keepdims=True)

    (spread,) = group_sums([chunked(chunks, square, zero_row)], per_group)
    inverse = lax.rsqrt(spread / count + EPSILON)
    gains = gain[...]

    def normalise(i, carry):
        value = (unit[rows_of(i), :] - average) * inverse
        unit[rows_of(i), :] = value
        normed[rows_of(i), :] = (value * gains).astype(jnp.bfloat16)
        return carry

    chunked(chunks, normalise, 0)

    loads[5].wait()
    query = dot(normed[own, :], qkv[:, :channels], 1, 0).astype(jnp.bfloat16)

    def project(i, highest):
        keyval[rows_of(i), :] = dot(normed[rows_of(i), :], qkv[:, channels:], 1, 0).astype(jnp.bfloat16)
        part = dot(keyval[rows_of(i), :channels], query, 1, 1) * scaling
        scores[rows_of(i), :] = part
        products[rows_of(i), :] = dot(keyval[rows_of(i), channels:], grad_att, 1, 1)
        return jnp.maximum(highest, jnp.max(part, axis=0, keepdims=True))

    highest = chunked(chunks, project, jnp.full((1, LANES), -jnp.inf, jnp.float32))

    def exponent(i, total):
        part = jnp.exp(scores[rows_of(i), :] - highest)
        scores[rows_of(i), :] = part
        return total + jnp.sum(part, axis=0, keepdims=True)

    share = 1.0 / chunked(chunks, exponent, jnp.zeros((1, LANES), jnp.float32))

    def normal(i, total):
        part = scores[rows_of(i), :] * share
        scores[rows_of(i), :] = part
        rounded = part.astype(jnp.bfloat16)
        soft[rows_of(i), :] = rounded
        return total + jnp.sum(rounded.astype(jnp.float32) * products[rows_of(i), :], axis=0, keepdims=True)

    delta = chunked(chunks, normal, jnp.zeros((1, LANES), jnp.float32))

    def backward(i, total):
        part = scores[rows_of(i), :] * (products[rows_of(i), :] - delta) * scaling
        rounded = part.astype(jnp.bfloat16)
        dscore[rows_of(i), :] = rounded
        grad_kv[rows_of(i), :channels] = dot(rounded, query, 1, 0).astype(jnp.bfloat16)
        grad_kv[rows_of(i), channels:] = dot(soft[rows_of(i), :], grad_att, 1, 0).astype(jnp.bfloat16)
        grad_norm[rows_of(i), :] = dot(grad_kv[rows_of(i), :], qkv[:, channels:], 1, 1)
        return total + dot(rounded, keyval[rows_of(i), :channels], 0, 0)

    grad_query = chunked(chunks, backward, jnp.zeros((LANES, channels), jnp.float32))
    grad_norm[own, :] += dot(grad_query.astype(jnp.bfloat16), qkv[:, :channels], 1, 1)

    def moments(i, carry):
        first, second = carry
        part = grad_norm[rows_of(i), :]
        first = first + jnp.sum(part, axis=0, keepdims=True)
        second = second + jnp.sum(part * unit[rows_of(i), :], axis=0, keepdims=True)
        return first, second

    first, second = chunked(chunks, moments, (zero_row, zero_row))
    first, second = group_sums([first * gains, second * gains], per_group)
    first = first / count
    second = second / count

    def hidden_grad(where):
        return (grad_norm[where, :] * gains - first - unit[where, :] * second) * inverse

    def finish(i, carry):
        grad_hid[rows_of(i), :] = hidden_grad(rows_of(i)).astype(jnp.bfloat16)
        return carry

    chunked(chunks, finish, 0)
    grad_hid[own, :] = (grad[...].astype(jnp.float32) + hidden_grad(own)).astype(jnp.bfloat16)

    columns[:, 0:LANES] = jnp.zeros((columns.shape[0], LANES), jnp.float32)
    columns[:, (rows + 1) * LANES :] = jnp.zeros((columns.shape[0], LANES), jnp.float32)

    def spread_taps(i, carry):
        if isinstance(i, int):
            where = pl.ds(LANES + i * chunk, chunk)
        else:
            where = pl.ds(pl.multiple_of(LANES + i * chunk, LANES), chunk)
        columns[:, where] = dot(conv[...], grad_hid[rows_of(i), :], 1, 1)
        return carry

    chunked(chunks, spread_taps, 0)

    def partial_copy(a, row, slot):
        return pltpu.make_async_remote_copy(
            src_ref=partial.at[a, row],
            dst_ref=arrived.at[a, slot],
            send_sem=part_send.at[a, row],
            recv_sem=part_recv.at[a, slot],
            device_id={"tm": t - a, "space": row},
            device_id_type=MESH,
        )

    for a in reversed(range(BACK)):
        for y in range(rows):
            total = jnp.zeros((lat_width, LANES), jnp.float32)
            for e in range(3):
                inner = jnp.zeros((lat_width, LANES), jnp.float32)
                for b in range(3):
                    tap = (a * 9 + b * 3 + e) * lat_width
                    at = (y - b + 2) * LANES
                    inner = inner + columns[tap : tap + lat_width, at : at + LANES]
                total = total + shifted(inner, 1 - e)
            partial[a, y] = total
        for d in range(rows):
            if a or d:

                @pl.when(t >= a)
                def _(a=a, d=d):
                    partial_copy(a, lax.rem(me + d, rows), me).start()

    arrived[0, me] = partial[0, me]
    for a in range(1, BACK):

        @pl.when(t + a >= frames)
        def _(a=a):
            arrived[a] = jnp.zeros(arrived.shape[1:], arrived.dtype)

    for a, d in pairs:

        @pl.when(t + a < frames)
        def _(a=a, d=d):
            slot = lax.rem(me + d, rows)
            partial_copy(a, slot, slot).wait_recv()

    total = jnp.zeros((lat_width, LANES), jnp.float32)
    for a in range(BACK):
        for r in range(rows):
            total = total + arrived[a, r]
    result_ref[...] = total

    for a, d in pairs:

        @pl.when(t + a < frames)
        def _(a=a, d=d):
            latent_copy(a, lax.rem(me + d, rows), me).wait_send()

        @pl.when(t >= a)
        def _(a=a, d=d):
            partial_copy(a, lax.rem(me + d, rows), me).wait_send()


def on_device(frames, rows, latent, conv_weight, norm_gain, qkv_weight, out_weight, grad_out):
    lat_width = latent.shape[1]
    channels = grad_out.shape[3]
    taps = 27 * lat_width
    cells = rows * LANES
    chunk = min(cells, 512)
    bf16, f32 = jnp.bfloat16, jnp.float32
    flat = (
        latent.reshape(lat_width, LANES),
        conv_weight.reshape(taps, channels),
        norm_gain.reshape(1, channels),
        qkv_weight,
        out_weight,
        grad_out.reshape(LANES, channels),
    )
    scratch = [pltpu.VMEM(value.shape, value.dtype) for value in flat]
    scratch += [
        pltpu.VMEM((BACK, rows, lat_width, LANES), bf16),
        pltpu.VMEM((taps, cells), bf16),
        pltpu.VMEM((cells, channels), f32),
        pltpu.VMEM((cells, channels), bf16),
        pltpu.VMEM((cells, 2 * channels), bf16),
        pltpu.VMEM((cells, LANES), f32),
        pltpu.VMEM((cells, LANES), f32),
        pltpu.VMEM((cells, LANES), bf16),
        pltpu.VMEM((cells, LANES), bf16),
        pltpu.VMEM((cells, 2 * channels), bf16),
        pltpu.VMEM((cells, channels), f32),
        pltpu.VMEM((cells, channels), bf16),
        pltpu.VMEM((taps, cells + 2 * LANES), f32),
        pltpu.VMEM((BACK, rows, lat_width, LANES), f32),
        pltpu.VMEM((BACK, rows, lat_width, LANES), f32),
        pltpu.SemaphoreType.DMA((6,)),
        pltpu.SemaphoreType.DMA((BACK, rows)),
        pltpu.SemaphoreType.DMA((BACK, rows)),
        pltpu.SemaphoreType.DMA((BACK, rows)),
        pltpu.SemaphoreType.DMA((BACK, rows)),
    ]
    result = pl.pallas_call(
        functools.partial(kernel, frames, rows, chunk),
        out_shape=jax.ShapeDtypeStruct((lat_width, LANES), f32),
        in_specs=[pl.BlockSpec(memory_space=pl.ANY)] * 6,
        out_specs=pl.BlockSpec(memory_space=pltpu.VMEM),
        scratch_shapes=scratch,
        compiler_params=pltpu.CompilerParams(
            collective_id=0, has_side_effects=True, vmem_limit_bytes=56 * 2**20
        ),
    )(*flat)
    return result.reshape(1, lat_width, 1, LANES)


def solution(mesh):
    return jax.shard_map(
        functools.partial(on_device, mesh.shape["tm"], mesh.shape["space"]),
        mesh=mesh,
        in_specs=(
            P(("group", "tm"), None, "space", None),
            P(),
            P(),
            P(),
            P(),
            P(("group", "tm"), "space", None, None),
        ),
        out_specs=P(("group", "tm"), None, "space", None),
        check_vma=False,
    )
```

time: 158 us -> 22.1 us (0.14)
  blocking collectives: 100 us -> 0 us
  Pallas kernels: 0 us -> 20.5 us
  waiting for transfers between devices: 18.7 us -> 0 us
  starting transfers between devices: 18.1 us -> 0 us
  matrix products: 9.75 us -> 0 us
  local copies, waits for them, and re-layouts: 7.57 us -> 1.3 us
  other arithmetic: 2.69 us -> 0 us
    all_gather x6 -> x0, blocking collectives: 77.8 us -> none  [the longest x1 15.7 us: on_device(): value_piece = lax.all_gather(value_part, 'space', axis=0, tiled=True)]
    psum x2 -> x0, blocking collectives: 22.6 us -> none  [the longest x1 12.6 us: on_device(): lax.psum((jnp.sum(grouped, axis=(0, 2)), jnp.sum(grouped * grouped, axis=...]
    pallas_call x0 -> x1, Pallas kernels: none -> 20.5 us  [on_device(): pl.pallas_call(functools.partial(kernel, frames, rows, chunk), out_shape=...]
    ppermute x8 -> x0, waiting for transfers between devices: 18.7 us -> none  [the longest x4 7.82 us: from_behind(): lax.ppermute(value, axis, [(source, source + steps) for source in range(l...]
    ppermute x8 -> x0, starting transfers between devices: 18.1 us -> none  [the longest x4 9.01 us: from_behind(): lax.ppermute(value, axis, [(source, source + steps) for source in range(l...]
    dot_general x13 -> x0, matrix products: 9.75 us -> none  [the longest x10 7.29 us: contract(): lax.dot_general(left, right, (((left_dim,), (right_dim,)), ((), ())), pre...]
    slice x6 -> x0, local copies, waits for them, and re-layouts: 2.11 us -> none  [the longest x1 0.74 us: on_device(): value_part = projected[:, 2 * channels:]]
  transfers between devices with their start and end apart: 8 -> 0, of which waited for: 7 -> 0; matrix products, arithmetic and copies ran while one was open for 3% -> 0% of each run, Pallas kernels for 0% -> 0%
where the time goes in v1:
time: 22.1 us; the launch traced here: 21.8 us
  Pallas kernels  20.5 us (93%)
  local copies, waits for them, and re-layouts  1.3 us (6%)
    pallas_call x1, Pallas kernels, on_device(): pl.pallas_call(functools.partial(kernel, frames, rows, chunk), out_shape=...  20.5 us
    unnamed x1, local copies, waits for them, and re-layouts  1.3 us

profile of v1, /device:TPU:0, one launch (start us, length us, event | category | flops | bytes accessed | tf_op | source)
XLA Modules:
  0.0 21.8 jit_solution(2338471914021617680)
XLA Ops:
  0.0 20.5 %shard_map.64 = f32[16,128]{1,0:T(8,128)} custom-call(bf16[16,128]{1,0:T(8,128)(2,1)} %bitcast.10, bf16[432,512]{1,0:T(8,128)(2,1)} %bitcast.7, f32[1,512]{1,0:T(1,128)} %bitcast.11, bf16[512,1536]{1,0:T(8,128)(2,1)} %qkv_hbm.1, bf16[512,512]{1,0:T(8,128)(2,1)} %out_hbm.1, bf16[128,512]{1,0:T(8,128)(2,1)} %bitcast.8), custom_call_target="tpu_custom_call" | custom-call | tf_op jit(solution)/shard_map/pallas_call | solution.py:360
  20.6 1.3 %copy.9 = f32[1,16,1,128]{3,2,1,0:T(1,128)} copy(f32[1,16,1,128]{3,2,1,0:T(1,128)} %bitcast.9) | data formatting | bytes 16384

commit v2 on v1

--- a/solution.py
+++ b/solution.py
@@ -58,7 +58,7 @@
     lat_hbm, conv_hbm, gain_hbm, qkv_hbm, out_hbm, grad_hbm,
     result_ref,
     lat, conv, gain, qkv, outw, grad,
-    window, patches, unit, normed, keyval, scores, products, soft, dscore, grad_kv, grad_norm,
+    window, patches, unit, normed, mixed, pair, scored, weights, grad_norm,
     grad_hid, columns, partial, arrived,
     load_sem, lat_send, lat_recv, part_send, part_recv,
 ):
@@ -75,25 +75,30 @@
     loads = [
         pltpu.make_async_copy(source, target, load_sem.at[i])
         for i, (source, target) in enumerate(
-            [(lat_hbm, lat), (grad_hbm, grad), (out_hbm, outw), (conv_hbm, conv), (gain_hbm, gain), (qkv_hbm, qkv)]
+            [(lat_hbm, lat), (grad_hbm, grad), (out_hbm, outw), (qkv_hbm, qkv), (conv_hbm, conv), (gain_hbm, gain)]
         )
     ]
-    for load in loads:
+    loads[0].start()
+
+    def other(k):
+        if k == rows - 1:
+            return me
+        upper = rows - 1 - k
+        return jnp.where(2 * me >= rows, jnp.where(k >= me, k + 1, k), jnp.where(upper <= me, upper - 1, upper))
+
+    barrier = pltpu.get_barrier_semaphore()
+    def greet(step):
+        for k in range(rows if step else rows - 1):
+            pl.semaphore_signal(
+                barrier, inc=1, device_id={"tm": t + step, "space": other(k)}, device_id_type=MESH
+            )
+
+    greet(0)
+    for step in range(1, BACK):
+        pl.when(t + step < frames)(functools.partial(greet, step))
+        pl.when(t >= step)(functools.partial(greet, -step))
+    for load in loads[1:]:
         load.start()
-
-    barrier = pltpu.get_barrier_semaphore()
-    for step in range(1 - BACK, BACK):
-        for d in range(rows):
-            if step == 0 and d == 0:
-                continue
-
-            @pl.when((t + step >= 0) & (t + step < frames))
-            def _(step=step, d=d):
-                pl.semaphore_signal(
-                    barrier, inc=1,
-                    device_id={"tm": t + step, "space": lax.rem(me + d, rows)},
-                    device_id_type=MESH,
-                )
 
     loads[0].wait()
     window[0, me] = lat[...]
@@ -106,33 +111,34 @@
     near = jnp.minimum(t, BACK - 1) + jnp.minimum(frames - 1 - t, BACK - 1) + 1
     pl.semaphore_wait(barrier, near * rows - 1)
 
-    def latent_copy(a, row, slot):
+    def send(source, target, send_sem, recv_sem, frame, row):
         return pltpu.make_async_remote_copy(
-            src_ref=lat,
-            dst_ref=window.at[a, slot],
-            send_sem=lat_send.at[a, row],
-            recv_sem=lat_recv.at[a, slot],
-            device_id={"tm": t + a, "space": row},
-            device_id_type=MESH,
+            src_ref=source, dst_ref=target, send_sem=send_sem, recv_sem=recv_sem,
+            device_id={"tm": frame, "space": row}, device_id_type=MESH,
         )
 
-    pairs = [(a, d) for a in range(BACK) for d in range(rows) if a or d]
-    for a, d in pairs:
-
-        @pl.when(t + a < frames)
-        def _(a=a, d=d):
-            latent_copy(a, lax.rem(me + d, rows), me).start()
+    def whole(buffer, a, send_sem, recv_sem):
+        block = buffer.at[a] if a else buffer.at[a, 0 : rows - 1]
+        return send(block, block, send_sem.at[a], recv_sem.at[a], t, me)
+
+    def send_latent(a):
+        for k in range(rows if a else rows - 1):
+            send(lat, window.at[a, me], lat_send.at[a], lat_recv.at[a], t + a, other(k)).start()
+
+    for a in reversed(range(BACK)):
+        pl.when(t + a < frames)(functools.partial(send_latent, a))
 
     loads[1].wait()
     loads[2].wait()
     grad_att = dot(grad[...], outw[...], 1, 1).astype(jnp.bfloat16)
-
-    for a, d in pairs:
-
-        @pl.when(t >= a)
-        def _(a=a, d=d):
-            slot = lax.rem(me + d, rows)
-            latent_copy(a, slot, slot).wait_recv()
+    loads[3].wait()
+    pair[LANES:, :] = dot(grad_att, qkv[:, 2 * channels :], 1, 1).astype(jnp.bfloat16)
+    mixed[...] = dot(qkv[:, :channels], qkv[:, channels : 2 * channels], 1, 1).astype(jnp.bfloat16)
+    loads[4].wait()
+    loads[5].wait()
+
+    for a in range(BACK):
+        pl.when(t >= a)(lambda a=a: whole(window, a, lat_send, lat_recv).wait_recv())
 
     zero_slab = jnp.zeros((3 * lat_width, LANES), jnp.bfloat16)
     for a in range(BACK):
@@ -150,9 +156,6 @@
         last = (a * 9 + 6) * lat_width
         patches[last : last + 3 * lat_width, (rows - 1) * LANES : rows * LANES] = zero_slab
 
-    loads[3].wait()
-    loads[4].wait()
-
     def rows_of(i):
         if isinstance(i, int):
             return pl.ds(i * chunk, chunk)
@@ -185,45 +188,40 @@
 
     chunked(chunks, normalise, 0)
 
-    loads[5].wait()
-    query = dot(normed[own, :], qkv[:, :channels], 1, 0).astype(jnp.bfloat16)
-
-    def project(i, highest):
-        keyval[rows_of(i), :] = dot(normed[rows_of(i), :], qkv[:, channels:], 1, 0).astype(jnp.bfloat16)
-        part = dot(keyval[rows_of(i), :channels], query, 1, 1) * scaling
-        scores[rows_of(i), :] = part
-        products[rows_of(i), :] = dot(keyval[rows_of(i), channels:], grad_att, 1, 1)
-        return jnp.maximum(highest, jnp.max(part, axis=0, keepdims=True))
-
-    highest = chunked(chunks, project, jnp.full((1, LANES), -jnp.inf, jnp.float32))
+    pair[:LANES, :] = dot(normed[own, :], mixed[...], 1, 0).astype(jnp.bfloat16)
+
+    def score(i, highest):
+        part = dot(normed[rows_of(i), :], pair[...], 1, 1)
+        scored[rows_of(i), :] = part
+        return jnp.maximum(highest, jnp.max(part[:, :LANES], axis=0, keepdims=True))
+
+    highest = chunked(chunks, score, jnp.full((1, LANES), -jnp.inf, jnp.float32))
 
     def exponent(i, total):
-        part = jnp.exp(scores[rows_of(i), :] - highest)
-        scores[rows_of(i), :] = part
+        part = jnp.exp((scored[rows_of(i), :LANES] - highest) * scaling)
+        scored[rows_of(i), :LANES] = part
         return total + jnp.sum(part, axis=0, keepdims=True)
 
     share = 1.0 / chunked(chunks, exponent, jnp.zeros((1, LANES), jnp.float32))
 
     def normal(i, total):
-        part = scores[rows_of(i), :] * share
-        scores[rows_of(i), :] = part
+        part = scored[rows_of(i), :LANES] * share
+        scored[rows_of(i), :LANES] = part
         rounded = part.astype(jnp.bfloat16)
-        soft[rows_of(i), :] = rounded
-        return total + jnp.sum(rounded.astype(jnp.float32) * products[rows_of(i), :], axis=0, keepdims=True)
+        weights[rows_of(i), LANES:] = rounded
+        return total + jnp.sum(rounded.astype(jnp.float32) * scored[rows_of(i), LANES:], axis=0, keepdims=True)
 
     delta = chunked(chunks, normal, jnp.zeros((1, LANES), jnp.float32))
 
     def backward(i, total):
-        part = scores[rows_of(i), :] * (products[rows_of(i), :] - delta) * scaling
+        part = scored[rows_of(i), :LANES] * (scored[rows_of(i), LANES:] - delta) * scaling
         rounded = part.astype(jnp.bfloat16)
-        dscore[rows_of(i), :] = rounded
-        grad_kv[rows_of(i), :channels] = dot(rounded, query, 1, 0).astype(jnp.bfloat16)
-        grad_kv[rows_of(i), channels:] = dot(soft[rows_of(i), :], grad_att, 1, 0).astype(jnp.bfloat16)
-        grad_norm[rows_of(i), :] = dot(grad_kv[rows_of(i), :], qkv[:, channels:], 1, 1)
-        return total + dot(rounded, keyval[rows_of(i), :channels], 0, 0)
-
-    grad_query = chunked(chunks, backward, jnp.zeros((LANES, channels), jnp.float32))
-    grad_norm[own, :] += dot(grad_query.astype(jnp.bfloat16), qkv[:, :channels], 1, 1)
+        weights[rows_of(i), :LANES] = rounded
+        grad_norm[rows_of(i), :] = dot(weights[rows_of(i), :], pair[...], 1, 0)
+        return total + dot(rounded, normed[rows_of(i), :], 0, 0)
+
+    pulled = chunked(chunks, backward, jnp.zeros((LANES, channels), jnp.float32))
+    grad_norm[own, :] += dot(pulled.astype(jnp.bfloat16), mixed[...], 1, 1)
 
     def moments(i, carry):
         first, second = carry
@@ -260,15 +258,10 @@
 
     chunked(chunks, spread_taps, 0)
 
-    def partial_copy(a, row, slot):
-        return pltpu.make_async_remote_copy(
-            src_ref=partial.at[a, row],
-            dst_ref=arrived.at[a, slot],
-            send_sem=part_send.at[a, row],
-            recv_sem=part_recv.at[a, slot],
-            device_id={"tm": t - a, "space": row},
-            device_id_type=MESH,
-        )
+    def send_partial(a):
+        for k in range(rows if a else rows - 1):
+            row = other(k)
+            send(partial.at[a, row], arrived.at[a, me], part_send.at[a], part_recv.at[a], t - a, row).start()
 
     for a in reversed(range(BACK)):
         for y in range(rows):
@@ -281,12 +274,7 @@
                     inner = inner + columns[tap : tap + lat_width, at : at + LANES]
                 total = total + shifted(inner, 1 - e)
             partial[a, y] = total
-        for d in range(rows):
-            if a or d:
-
-                @pl.when(t >= a)
-                def _(a=a, d=d):
-                    partial_copy(a, lax.rem(me + d, rows), me).start()
+        pl.when(t >= a)(functools.partial(send_partial, a))
 
     arrived[0, me] = partial[0, me]
     for a in range(1, BACK):
@@ -295,12 +283,8 @@
         def _(a=a):
             arrived[a] = jnp.zeros(arrived.shape[1:], arrived.dtype)
 
-    for a, d in pairs:
-
-        @pl.when(t + a < frames)
-        def _(a=a, d=d):
-            slot = lax.rem(me + d, rows)
-            partial_copy(a, slot, slot).wait_recv()
+    for a in range(BACK):
+        pl.when(t + a < frames)(lambda a=a: whole(arrived, a, part_send, part_recv).wait_recv())
 
     total = jnp.zeros((lat_width, LANES), jnp.float32)
     for a in range(BACK):
@@ -308,15 +292,9 @@
             total = total + arrived[a, r]
     result_ref[...] = total
 
-    for a, d in pairs:
-
-        @pl.when(t + a < frames)
-        def _(a=a, d=d):
-            latent_copy(a, lax.rem(me + d, rows), me).wait_send()
-
-        @pl.when(t >= a)
-        def _(a=a, d=d):
-            partial_copy(a, lax.rem(me + d, rows), me).wait_send()
+    for a in range(BACK):
+        pl.when(t + a < frames)(lambda a=a: whole(window, a, lat_send, lat_recv).wait_send())
+        pl.when(t >= a)(lambda a=a: whole(partial, a, part_send, part_recv).wait_send())
 
 
 def on_device(frames, rows, latent, conv_weight, norm_gain, qkv_weight, out_weight, grad_out):
@@ -340,22 +318,20 @@
         pltpu.VMEM((taps, cells), bf16),
         pltpu.VMEM((cells, channels), f32),
         pltpu.VMEM((cells, channels), bf16),
-        pltpu.VMEM((cells, 2 * channels), bf16),
-        pltpu.VMEM((cells, LANES), f32),
-        pltpu.VMEM((cells, LANES), f32),
-        pltpu.VMEM((cells, LANES), bf16),
-        pltpu.VMEM((cells, LANES), bf16),
-        pltpu.VMEM((cells, 2 * channels), bf16),
+        pltpu.VMEM((channels, channels), bf16),
+        pltpu.VMEM((2 * LANES, channels), bf16),
+        pltpu.VMEM((cells, 2 * LANES), f32),
+        pltpu.VMEM((cells, 2 * LANES), bf16),
         pltpu.VMEM((cells, channels), f32),
         pltpu.VMEM((cells, channels), bf16),
         pltpu.VMEM((taps, cells + 2 * LANES), f32),
         pltpu.VMEM((BACK, rows, lat_width, LANES), f32),
         pltpu.VMEM((BACK, rows, lat_width, LANES), f32),
         pltpu.SemaphoreType.DMA((6,)),
-        pltpu.SemaphoreType.DMA((BACK, rows)),
-        pltpu.SemaphoreType.DMA((BACK, rows)),
-        pltpu.SemaphoreType.DMA((BACK, rows)),
-        pltpu.SemaphoreType.DMA((BACK, rows)),
+        pltpu.SemaphoreType.DMA((BACK,)),
+        pltpu.SemaphoreType.DMA((BACK,)),
+        pltpu.SemaphoreType.DMA((BACK,)),
+        pltpu.SemaphoreType.DMA((BACK,)),
     ]
     result = pl.pallas_call(
         functools.partial(kernel, frames, rows, chunk),

time: 22.1 us -> 20.6 us (0.932)
  Pallas kernels: 20.5 us -> 19.1 us
    pallas_call x1, Pallas kernels: 20.5 us -> 19.1 us  [on_device(): pl.pallas_call(functools.partial(kernel, frames, rows, chunk), out_shape=...]
where the time goes in v2:
time: 20.6 us; the launch traced here: 20.4 us
  Pallas kernels  19.1 us (93%)
  local copies, waits for them, and re-layouts  1.3 us (6%)
    pallas_call x1, Pallas kernels, on_device(): pl.pallas_call(functools.partial(kernel, frames, rows, chunk), out_shape=...  19.1 us
    unnamed x1, local copies, waits for them, and re-layouts  1.3 us

profile of v2, /device:TPU:0, one launch (start us, length us, event | category | flops | bytes accessed | tf_op | source)
XLA Modules:
  0.0 20.4 jit_solution(7720379039834921391)
XLA Ops:
  0.0 19.1 %shard_map.64 = f32[16,128]{1,0:T(8,128)} custom-call(bf16[16,128]{1,0:T(8,128)(2,1)} %bitcast.10, bf16[432,512]{1,0:T(8,128)(2,1)} %bitcast.7, f32[1,512]{1,0:T(1,128)} %bitcast.11, bf16[512,1536]{1,0:T(8,128)(2,1)} %qkv_hbm.1, bf16[512,512]{1,0:T(8,128)(2,1)} %out_hbm.1, bf16[128,512]{1,0:T(8,128)(2,1)} %bitcast.8), custom_call_target="tpu_custom_call" | custom-call | tf_op jit(solution)/shard_map/pallas_call | solution.py:336
  19.1 1.3 %copy.9 = f32[1,16,1,128]{3,2,1,0:T(1,128)} copy(f32[1,16,1,128]{3,2,1,0:T(1,128)} %bitcast.9) | data formatting | bytes 16384

commit v3 on v2

--- a/solution.py
+++ b/solution.py
@@ -58,7 +58,7 @@
     lat_hbm, conv_hbm, gain_hbm, qkv_hbm, out_hbm, grad_hbm,
     result_ref,
     lat, conv, gain, qkv, outw, grad,
-    window, patches, unit, normed, mixed, pair, scored, weights, grad_norm,
+    window, patches, hidden, normed, mixed, pair, scored, weights, grad_norm,
     grad_hid, columns, partial, arrived,
     load_sem, lat_send, lat_recv, part_send, part_recv,
 ):
@@ -121,12 +121,12 @@
         block = buffer.at[a] if a else buffer.at[a, 0 : rows - 1]
         return send(block, block, send_sem.at[a], recv_sem.at[a], t, me)
 
-    def send_latent(a):
-        for k in range(rows if a else rows - 1):
-            send(lat, window.at[a, me], lat_send.at[a], lat_recv.at[a], t + a, other(k)).start()
-
-    for a in reversed(range(BACK)):
-        pl.when(t + a < frames)(functools.partial(send_latent, a))
+    def send_latent(a, k):
+        send(lat, window.at[a, me], lat_send.at[a], lat_recv.at[a], t + a, other(k)).start()
+
+    for k in range(rows):
+        for a in reversed(range(0 if k < rows - 1 else 1, BACK)):
+            pl.when(t + a < frames)(functools.partial(send_latent, a, k))
 
     loads[1].wait()
     loads[2].wait()
@@ -165,7 +165,7 @@
 
     def convolve(i, total):
         part = dot(patches[:, rows_of(i)], conv[...], 0, 0)
-        unit[rows_of(i), :] = part
+        hidden[rows_of(i), :] = part
         return total + jnp.sum(part, axis=0, keepdims=True)
 
     count = float(cells * per_group)
@@ -173,17 +173,17 @@
     average = average / count
 
     def square(i, total):
-        away = unit[rows_of(i), :] - average
+        away = hidden[rows_of(i), :] - average
         return total + jnp.sum(away * away, axis=0, keepdims=True)
 
     (spread,) = group_sums([chunked(chunks, square, zero_row)], per_group)
     inverse = lax.rsqrt(spread / count + EPSILON)
     gains = gain[...]
 
+    slope = inverse * gains
+
     def normalise(i, carry):
-        value = (unit[rows_of(i), :] - average) * inverse
-        unit[rows_of(i), :] = value
-        normed[rows_of(i), :] = (value * gains).astype(jnp.bfloat16)
+        normed[rows_of(i), :] = ((hidden[rows_of(i), :] - average) * slope).astype(jnp.bfloat16)
         return carry
 
     chunked(chunks, normalise, 0)
@@ -227,16 +227,19 @@
         first, second = carry
         part = grad_norm[rows_of(i), :]
         first = first + jnp.sum(part, axis=0, keepdims=True)
-        second = second + jnp.sum(part * unit[rows_of(i), :], axis=0, keepdims=True)
+        second = second + jnp.sum(part * (hidden[rows_of(i), :] - average), axis=0, keepdims=True)
         return first, second
 
     first, second = chunked(chunks, moments, (zero_row, zero_row))
-    first, second = group_sums([first * gains, second * gains], per_group)
+    first, second = group_sums([first * gains, second * slope], per_group)
     first = first / count
     second = second / count
 
+    tilt = second * inverse * inverse
+    offset = average * tilt - first * inverse
+
     def hidden_grad(where):
-        return (grad_norm[where, :] * gains - first - unit[where, :] * second) * inverse
+        return grad_norm[where, :] * slope - hidden[where, :] * tilt + offset
 
     def finish(i, carry):
         grad_hid[rows_of(i), :] = hidden_grad(rows_of(i)).astype(jnp.bfloat16)
@@ -335,7 +338,7 @@
     ]
     result = pl.pallas_call(
         functools.partial(kernel, frames, rows, chunk),
-        out_shape=jax.ShapeDtypeStruct((lat_width, LANES), f32),
+        out_shape=pltpu.VMEM((lat_width, LANES), f32),
         in_specs=[pl.BlockSpec(memory_space=pl.ANY)] * 6,
         out_specs=pl.BlockSpec(memory_space=pltpu.VMEM),
         scratch_shapes=scratch,

time: 20.6 us -> 19.1 us (0.927)
  Pallas kernels: 19.1 us -> 18.3 us
  local copies, waits for them, and re-layouts: 1.3 us -> 0.6 us
    pallas_call x1, Pallas kernels: 19.1 us -> 18.3 us  [on_device(): pl.pallas_call(functools.partial(kernel, frames, rows, chunk), out_shape=...]
    unnamed x1, local copies, waits for them, and re-layouts: 1.3 us -> 0.6 us
where the time goes in v3:
time: 19.1 us; the launch traced here: 18.9 us
  Pallas kernels  18.3 us (96%)
  local copies, waits for them, and re-layouts  0.6 us (3%)
    pallas_call x1, Pallas kernels, on_device(): pl.pallas_call(functools.partial(kernel, frames, rows, chunk), out_shape=...  18.3 us
    unnamed x1, local copies, waits for them, and re-layouts  0.6 us

profile of v3, /device:TPU:0, one launch (start us, length us, event | category | flops | bytes accessed | tf_op | source)
XLA Modules:
  0.0 18.9 jit_solution(12883809972429525725)
XLA Ops:
  0.0 18.3 %shard_map.64 = f32[16,128]{1,0:T(8,128)S(1)} custom-call(bf16[16,128]{1,0:T(8,128)(2,1)} %bitcast.10, bf16[432,512]{1,0:T(8,128)(2,1)} %bitcast.8, f32[1,512]{1,0:T(1,128)} %bitcast.11, bf16[512,1536]{1,0:T(8,128)(2,1)} %qkv_hbm.1, bf16[512,512]{1,0:T(8,128)(2,1)} %out_hbm.1, bf16[128,512]{1,0:T(8,128)(2,1)} %bitcast.9), custom_call_target="tpu_custom_call" | custom-call | tf_op jit(solution)/shard_map/pallas_call | solution.py:339
  18.3 0.6 %copy.9 = f32[1,16,1,128]{3,2,1,0:T(1,128)} copy(f32[1,16,1,128]{3,2,1,0:T(1,128)S(1)} %bitcast.7) | data formatting | bytes 16384

commit v4 on v3

--- a/solution.py
+++ b/solution.py
@@ -48,8 +48,10 @@
 
 
 def chunked(count, body, carry):
-    if count == 1:
-        return body(0, carry)
+    if count <= 4:
+        for i in range(count):
+            carry = body(i, carry)
+        return carry
     return lax.fori_loop(0, count, body, carry)
 
 
@@ -305,7 +307,7 @@
     channels = grad_out.shape[3]
     taps = 27 * lat_width
     cells = rows * LANES
-    chunk = min(cells, 512)
+    chunk = min(cells, 256)
     bf16, f32 = jnp.bfloat16, jnp.float32
     flat = (
         latent.reshape(lat_width, LANES),

time: 19.1 us -> 18.8 us (0.984)
  Pallas kernels: 18.3 us -> 18 us
    pallas_call x1, Pallas kernels: 18.3 us -> 18 us  [on_device(): pl.pallas_call(functools.partial(kernel, frames, rows, chunk), out_shape=...]
where the time goes in v4:
time: 18.8 us; the launch traced here: 18.6 us
  Pallas kernels  18 us (96%)
  local copies, waits for them, and re-layouts  0.6 us (3%)
    pallas_call x1, Pallas kernels, on_device(): pl.pallas_call(functools.partial(kernel, frames, rows, chunk), out_shape=...  18 us
    unnamed x1, local copies, waits for them, and re-layouts  0.6 us

profile of v4, /device:TPU:0, one launch (start us, length us, event | category | flops | bytes accessed | tf_op | source)
XLA Modules:
  0.0 18.6 jit_solution(12355045457005983443)
XLA Ops:
  0.0 18.0 %shard_map.64 = f32[16,128]{1,0:T(8,128)S(1)} custom-call(bf16[16,128]{1,0:T(8,128)(2,1)} %bitcast.10, bf16[432,512]{1,0:T(8,128)(2,1)} %bitcast.8, f32[1,512]{1,0:T(1,128)} %bitcast.11, bf16[512,1536]{1,0:T(8,128)(2,1)} %qkv_hbm.1, bf16[512,512]{1,0:T(8,128)(2,1)} %out_hbm.1, bf16[128,512]{1,0:T(8,128)(2,1)} %bitcast.9), custom_call_target="tpu_custom_call" | custom-call | tf_op jit(solution)/shard_map/pallas_call | solution.py:341
  18.0 0.6 %copy.9 = f32[1,16,1,128]{3,2,1,0:T(1,128)} copy(f32[1,16,1,128]{3,2,1,0:T(1,128)S(1)} %bitcast.7) | data formatting | bytes 16384
